TPU v7x, 512 devices: a whole 4x4x16 slice. The times are simulated.
512 devices in a mesh: ctx: 16 (over x, y), ep: 32 (over z, core).
Axes of the slice: x: 4, y: 4, z: 16, core: 2. Of those that a mesh axis runs over, the one named last changes fastest.
Arguments:
- queries: bfloat16 [32, 2048, 4096], P('ep', 'ctx'), may hold values from -7 to 7
- keys: bfloat16 [32, 2048, 256], P('ep', 'ctx'), may hold values from -4.5 to 4.5
- values: bfloat16 [32, 2048, 256], P('ep', 'ctx'), may hold values from -5 to 5
- hidden: bfloat16 [32, 2048, 2048], P('ep', 'ctx'), may hold values from -130 to 130
- expert_ids: int32 [32, 2048, 2], P('ep', 'ctx'), may hold values from 0 to 31, all different within a row; in each aligned block of 128 rows (0 to 127, 128 to 255, ..., all dimensions but the last counted through in order) at most 12 rows name the same one
- gate_probs: float32 [32, 2048, 2], P('ep', 'ctx'), may hold values from 0.2 to 1
- norm_gain: float32 [2048], replicated, may hold values from 0.1 to 1.9
- w_gate: bfloat16 [32, 768, 2048], P('ep', 'ctx'), may hold values from -0.125 to 0.125
- w_up: bfloat16 [32, 768, 2048], P('ep', 'ctx'), may hold values from -0.125 to 0.125
- w_down: bfloat16 [32, 768, 2048], P('ep', 'ctx'), may hold values from -0.21875 to 0.21875
Outputs:
- attended: bfloat16 [32, 2048, 4096], P('ep', 'ctx')
- expert_mix: bfloat16 [32, 2048, 2048], P('ep', 'ctx')
Inputs may be any that keep to these rules, and one draw needn't show every extreme that they name: `expert_ids`: the 2 experts of one token differ. Among the 128 tokens of one device no expert is named more than 12 times.
All inputs are finite; a program needn't handle non-finite values.
Results may differ from a plain program's by a relative error of at most 0.0071.
Values may be sent and summed in bfloat16 or wider, within the bound.
No kernel may reach another device: no remote copies, remote signals or barrier semaphores. Data moves between devices by JAX's collectives and lax.ppermute only.
A program may use at most 128 MiB of HBM per device.

v0:
```python
import math
import jax
import jax.numpy as jnp
from jax import lax
from jax.sharding import PartitionSpec as P

HQ = 32
KVH = 2
DH = 128


def attend(queries, keys, values):
    row_count = queries.shape[1]
    head_ratio = HQ // KVH
    score_factor = 1.0 / math.sqrt(DH)
    my_index = lax.axis_index("ctx")
    query_heads = queries[0].reshape(row_count, KVH, head_ratio, DH)
    groups = [(query_heads, my_index * row_count + jnp.arange(row_count, dtype=jnp.int32))]
    initial = tuple(
        (
            (
                jnp.full((KVH, head_ratio, group_rows.shape[0]), -1e30, jnp.float32),
                jnp.zeros((KVH, head_ratio, group_rows.shape[0]), jnp.float32),
                jnp.zeros((KVH, head_ratio, group_rows.shape[0], DH), jnp.float32),
            )
            for group_rows, group_pos in groups
        )
    )

    def update(carried, pieces_in, offset):
        key_piece, value_piece = pieces_in
        piece_rows = key_piece.shape[0]
        key_heads = key_piece.reshape(piece_rows, KVH, DH)
        value_heads = value_piece.reshape(piece_rows, KVH, DH)
        key_pos = jnp.arange(piece_rows, dtype=jnp.int32)
        updated = []
        for (group_rows, query_pos), current in zip(groups, carried):

            def compute(present, group_rows=group_rows, query_pos=query_pos):
                maxima, totals, weighted = present
                scores = (
                    jnp.einsum(
                        "rgjd,ngd->gjrn", group_rows, key_heads, preferred_element_type=jnp.float32
                    )
                    * score_factor
                )
                visible = key_pos[None, :] <= query_pos[:, None]
                scores = jnp.where(visible, scores, -jnp.inf)
                new_maxima = jnp.maximum(maxima, jnp.max(scores, axis=-1))
                exponent = jnp.exp(scores - new_maxima[..., None])
                new_totals = jnp.sum(exponent, axis=-1)
                product = jnp.einsum(
                    "gjrn,ngd->gjrd",
                    exponent.astype(jnp.bfloat16),
                    value_heads,
                    preferred_element_type=jnp.float32,
                )
                return (new_maxima, new_totals, product)

            def unchanged(present):
                return present

            updated.append(lax.cond(offset <= jnp.max(query_pos), compute, unchanged, current))
        return tuple(updated)

    finals = update(
        initial,
        (
            lax.all_gather(keys[0], "ctx", axis=0, tiled=True),
            lax.all_gather(values[0], "ctx", axis=0, tiled=True),
        ),
        jnp.int32(0),
    )
    outputs = []
    for (group_rows, query_pos), final_state in zip(groups, finals):
        maxima, totals, weighted = final_state
        result = weighted / totals[..., None]
        result = jnp.transpose(result, (2, 0, 1, 3)).reshape(group_rows.shape[0], HQ * DH)
        outputs.append(result.astype(jnp.bfloat16))
    merged = outputs[0]
    return merged[None]


def experts(hidden, expert_ids, gate_probs, norm_gain, w_gate, w_up, w_down):
    tokens = hidden[0].astype(jnp.float32)
    row_count = tokens.shape[0]
    route_count = expert_ids.shape[2]
    expert_count = lax.axis_size("ep")
    capacity = 3 * row_count * route_count // (2 * expert_count)
    mean_square = jnp.mean(tokens * tokens, axis=-1, keepdims=True)
    normed = (tokens * lax.rsqrt(mean_square + 1e-06) * norm_gain).astype(jnp.bfloat16)
    flat_ids = expert_ids[0].reshape(row_count * route_count)
    onehot = (flat_ids[:, None] == jnp.arange(expert_count, dtype=jnp.int32)[None, :]).astype(
        jnp.int32
    )
    before = jnp.cumsum(onehot, axis=0) - onehot
    slot_index = jnp.sum(before * onehot, axis=1)
    target = (flat_ids * capacity + slot_index).reshape(row_count, route_count)
    slot_rows = jnp.arange(expert_count * capacity, dtype=jnp.int32)
    placement = jnp.any(target[None, :, :] == slot_rows[:, None, None], axis=-1).astype(
        jnp.bfloat16
    )
    outgoing = jnp.dot(placement, normed, preferred_element_type=jnp.float32).astype(jnp.bfloat16)
    outgoing = outgoing.reshape(expert_count, capacity, normed.shape[1])
    received = lax.all_to_all(outgoing, "ep", split_axis=0, concat_axis=0, tiled=True)
    flat_rows = received.reshape(expert_count * capacity, normed.shape[1])
    gate_rows = lax.all_gather(w_gate[0], "ctx", axis=0, tiled=True)
    up_rows = lax.all_gather(w_up[0], "ctx", axis=0, tiled=True)
    down_rows = lax.all_gather(w_down[0], "ctx", axis=0, tiled=True)
    contract = (((1,), (1,)), ((), ()))
    gate_pre = lax.dot_general(flat_rows, gate_rows, contract, preferred_element_type=jnp.float32)
    up_pre = lax.dot_general(flat_rows, up_rows, contract, preferred_element_type=jnp.float32)
    activated = (jax.nn.silu(gate_pre) * up_pre).astype(jnp.bfloat16)
    produced = jnp.dot(activated, down_rows, preferred_element_type=jnp.float32)
    produced = produced.astype(jnp.bfloat16).reshape(expert_count, capacity, normed.shape[1])
    returned = lax.all_to_all(produced, "ep", split_axis=0, concat_axis=0, tiled=True)
    returned_rows = returned.reshape(expert_count * capacity, normed.shape[1])
    picked = returned_rows[target]
    route_weight = gate_probs[0]
    mixture = jnp.zeros((row_count, normed.shape[1]), jnp.float32)
    for route in range(route_count):
        mixture = mixture + route_weight[:, route : route + 1] * picked[:, route].astype(
            jnp.float32
        )
    return mixture.astype(jnp.bfloat16)[None]


def per_device(
    queries, keys, values, hidden, expert_ids, gate_probs, norm_gain, w_gate, w_up, w_down
):
    attended = attend(queries, keys, values)
    expert_mix = experts(hidden, expert_ids, gate_probs, norm_gain, w_gate, w_up, w_down)
    return (attended, expert_mix)


def solution(mesh):
    placed = (
        P("ep", "ctx", None),
        P("ep", "ctx", None),
        P("ep", "ctx", None),
        P("ep", "ctx", None),
        P("ep", "ctx", None),
        P("ep", "ctx", None),
        P(),
        P("ep", "ctx", None),
        P("ep", "ctx", None),
        P("ep", "ctx", None),
    )
    return jax.shard_map(
        per_device,
        mesh=mesh,
        in_specs=placed,
        out_specs=(P("ep", "ctx", None), P("ep", "ctx", None)),
        check_vma=False,
    )
```

profile of v0, /device:TPU:32, one launch (start us, length us, event | category | flops | bytes accessed | tf_op | source)
XLA Modules:
  0.0 414.3 jit_solution(6666725445391555825)
XLA Ops:
  11.0 1.2 fusion.27
  12.2 1.7 convolution_convert_fusion
  13.9 1.5 reshape.198
  15.4 15.3 %all-to-all-start = ((bf16[32,12,2048]{2,1,0:T(8,128)(2,1)}), bf16[32,12,2048]{2,1,0:T(8,128)(2,1)S(1)}, u32[]{:S(2)}, u32[]{:S(2)}) async-start(bf16[32,12,2048]{2,1,0:T(8,128)(2,1)} %reshape.198), calls=%async_computation | async-start | bytes 4194304 | tf_op jit(solution)/shard_map/all_to_all | solution.py:105
  31.5 99.4 %all-to-all-done = bf16[32,12,2048]{2,1,0:T(8,128)(2,1)S(1)} async-done(((bf16[32,12,2048]{2,1,0:T(8,128)(2,1)}), bf16[32,12,2048]{2,1,0:T(8,128)(2,1)S(1)}, u32[]{:S(2)}, u32[]{:S(2)}) %all-to-all-start) | async-done | bytes 1572896 | tf_op jit(solution)/shard_map/all_to_all | solution.py:105
  130.9 1.4 reshape.199
  132.3 5.1 %fusion.16 = f32[384,768]{1,0:T(8,128)} fusion(bf16[384,2048]{1,0:T(8,128)(2,1)} %reshape.199, bf16[1,768,2048]{2,1,0:T(8,128)(2,1)} %all-gather.15.cloned.1.call-done), kind=kOutput, calls=%fused_computation.20 | convolution fusion | flops 1207959552 | bytes 5898240 | tf_op jit(solution)/shard_map/dot_general | solution.py:111
  137.3 6.5 %all-gather.19.cloned.1.call-done = bf16[1,768,2048]{2,1,0:T(8,128)(2,1)} async-done(((bf16[1,48,2048]{2,1,0:T(8,128)(2,1)}), bf16[1,768,2048]{2,1,0:T(8,128)(2,1)}) %all-gather.19.cloned.1.call-update) | async-done | bytes 3145744 | tf_op jit(solution)/shard_map/all_gather | solution.py:109
  143.8 65.4 %all-gather.17.cloned.1.call-done = bf16[1,768,2048]{2,1,0:T(8,128)(2,1)} async-done(((bf16[1,48,2048]{2,1,0:T(8,128)(2,1)}), bf16[1,768,2048]{2,1,0:T(8,128)(2,1)}) %all-gather.17.cloned.1.call-update) | async-done | bytes 3145744 | tf_op jit(solution)/shard_map/all_gather | solution.py:108
  209.2 6.3 %fusion.18 = bf16[384,2048]{1,0:T(8,128)(2,1)S(1)} fusion(bf16[1,768,2048]{2,1,0:T(8,128)(2,1)} %all-gather.19.cloned.1.call-done, bf16[384,2048]{1,0:T(8,128)(2,1)S(1)} %copy-done, bf16[1,768,2048]{2,1,0:T(8,128)(2,1)} %all-gather.17.cloned.1.call-done, f32[384,768]{1,0:T(8,128)} %fusion.16), kind=kOutput, calls=%fused_computation.22 | convolution fusion | flops 2418475008 | bytes 10616832 | tf_op jit(solution)/shard_map/dot_general | solution.py:114
  215.5 1.6 reshape.200
  217.1 13.0 %all-to-all-start.1 = ((bf16[32,12,2048]{2,1,0:T(8,128)(2,1)}), bf16[32,12,2048]{2,1,0:T(8,128)(2,1)}, u32[]{:S(2)}, u32[]{:S(2)}) async-start(bf16[32,12,2048]{2,1,0:T(8,128)(2,1)} %reshape.200), calls=%async_computation.1 | async-start | bytes 4194304 | tf_op jit(solution)/shard_map/all_to_all | solution.py:116
  232.9 57.1 %all-gather.11.cloned.1.call-done = bf16[1,2048,256]{2,1,0:T(8,128)(2,1)} async-done(((bf16[1,128,256]{2,1,0:T(8,128)(2,1)}), bf16[1,2048,256]{2,1,0:T(8,128)(2,1)}) %all-gather.11.cloned.1.call-update) | async-done | bytes 1048592 | tf_op jit(solution)/shard_map/all_gather | solution.py:69
  289.9 60.4 %all-gather.13.cloned.1.call-done = bf16[1,2048,256]{2,1,0:T(8,128)(2,1)} async-done(((bf16[1,128,256]{2,1,0:T(8,128)(2,1)}), bf16[1,2048,256]{2,1,0:T(8,128)(2,1)}) %all-gather.13.cloned.1.call-update) | async-done | bytes 1048592 | tf_op jit(solution)/shard_map/all_gather | solution.py:70
  350.3 46.9 %conditional.1 = (f32[2,16,128]{2,1,0:T(8,128)S(1)}, f32[2,16,128,128]{3,2,1,0:T(8,128)S(1)}) conditional(s32[]{:T(128)} %convert_element_type.84, () %tuple.16, (s32[2048]{0:T(1024)S(1)}, s32[128]{0:T(128)S(1)}, bf16[2048,256]{1,0:T(8,128)(2,1)}, bf16[1,128,4096]{2,1,0:T(8,128)(2,1)S(1)}, bf16[2048,256]{1,0:T(8,128)(2,1)}) %tuple.36), branch_computations={%region_1.0_spmd, %region_2.5_spmd} | conditional | flops 4387500032 | bytes 117547560 | solution.py:63
  350.9 1.3 reshape.190
  352.3 13.2 %fusion.2 = (f32[2,16,128]{2,1,0:T(8,128)S(1)}, f32[2,2048,128,16]{2,1,3,0:T(8,128)}) fusion(pred[128,2048]{0,1:T(8,128)(4,1)S(1)} %broadcast_compare_fusion, bf16[128,2,16,128]{3,2,1,0:T(8,128)(2,1)S(1)} %bitcast.90, bf16[2048,2,128,1]{2,1,0,3:T(2,128)(2,1)S(1)} %bitcast.91), kind=kOutput, calls=%fused_computation.5 | convolution fusion | flops 2172645376 | bytes 35930112 | tf_op jit(solution)/shard_map/cond/branch_1_fun/rgjd,ngd->gjrn/dot_general | solution.py:42
  365.5 14.4 %fusion.1 = f32[2,16,128]{2,1,0:T(8,128)S(1)} fusion(f32[2,2048,128,16]{2,1,3,0:T(8,128)} %get-tuple-element.27, f32[2,16,128]{2,1,0:T(8,128)S(1)} %broadcast_maximum_fusion, pred[128,2048]{0,1:T(8,128)(4,1)S(1)} %broadcast_compare_fusion), kind=kLoop, calls=%fused_computation.4 | loop fusion | flops 33550336 | bytes 33849344 | tf_op jit(solution)/shard_map/cond/branch_1_fun/reduce_sum | solution.py:51
  381.0 15.9 %fusion.3 = f32[2,16,128,128]{3,2,1,0:T(8,128)S(1)} fusion(f32[2,2048,128,16]{2,1,3,0:T(8,128)} %get-tuple-element.27, f32[2,16,128]{2,1,0:T(8,128)S(1)} %broadcast_maximum_fusion, pred[128,2048]{0,1:T(8,128)(4,1)S(1)} %broadcast_compare_fusion, bf16[2048,2,128,1]{2,1,0,3:T(2,128)(2,1)} %bitcast.95), kind=kOutput, calls=%fused_computation.6 | convolution fusion | flops 2181038080 | bytes 36978688 | tf_op jit(solution)/shard_map/cond/branch_1_fun/gjrn,ngd->gjrd/dot_general | solution.py:52
  398.6 1.3 convert_element_type.87
  399.9 2.5 reshape.201
  402.4 1.4 gather_fusion
  404.5 1.5 fusion.47
  406.0 1.8 fusion.31
  (49 shorter events, 10.4 us)
Async XLA Ops:
  7.2 125.1 %all-gather.15.cloned.1.call-start = ((), (), s32[]{:S(2)}) async-start(), calls=%async_computation.4 | async-start | bytes 3342336 | tf_op jit(solution)/shard_map/all_gather | solution.py:107
  7.9 135.9 %all-gather.19.cloned.1.call-start = ((), (), s32[]{:S(2)}) async-start(), calls=%async_computation.6 | async-start | bytes 3342336 | tf_op jit(solution)/shard_map/all_gather | solution.py:109
  15.4 115.5 %all-to-all-start = ((bf16[32,12,2048]{2,1,0:T(8,128)(2,1)}), bf16[32,12,2048]{2,1,0:T(8,128)(2,1)S(1)}, u32[]{:S(2)}, u32[]{:S(2)}) async-start(bf16[32,12,2048]{2,1,0:T(8,128)(2,1)} %reshape.198), calls=%async_computation | async-start | bytes 4194304 | tf_op jit(solution)/shard_map/all_to_all | solution.py:105
  30.8 178.5 %all-gather.17.cloned.1.call-start = ((), (), s32[]{:S(2)}) async-start(), calls=%async_computation.5 | async-start | bytes 3342336 | tf_op jit(solution)/shard_map/all_gather | solution.py:108
  132.3 77.0 %copy-start = (bf16[384,2048]{1,0:T(8,128)(2,1)S(1)}, bf16[384,2048]{1,0:T(8,128)(2,1)}, u32[]{:S(2)}) copy-start(bf16[384,2048]{1,0:T(8,128)(2,1)} %reshape.199) | copy-start | bytes 4718596
  217.1 15.8 %copy-start.3 = (f32[1,128,2]{1,2,0:T(2,128)S(1)}, f32[1,128,2]{1,2,0:T(2,128)}, u32[]{:S(2)}) copy-start(f32[1,128,2]{1,2,0:T(2,128)} %param.17) | copy-start | bytes 3076
  217.1 133.3 %copy-start.1 = (bf16[1,128,4096]{2,1,0:T(8,128)(2,1)S(1)}, bf16[1,128,4096]{2,1,0:T(8,128)(2,1)}, u32[]{:S(2)}) copy-start(bf16[1,128,4096]{2,1,0:T(8,128)(2,1)} %param.12) | copy-start | bytes 3145732
  217.1 182.8 %all-to-all-start.1 = ((bf16[32,12,2048]{2,1,0:T(8,128)(2,1)}), bf16[32,12,2048]{2,1,0:T(8,128)(2,1)}, u32[]{:S(2)}, u32[]{:S(2)}) async-start(bf16[32,12,2048]{2,1,0:T(8,128)(2,1)} %reshape.200), calls=%async_computation.1 | async-start | bytes 4194304 | tf_op jit(solution)/shard_map/all_to_all | solution.py:116
  230.1 59.9 %all-gather.11.cloned.1.call-start = ((), (), s32[]{:S(2)}) async-start(), calls=%async_computation.2 | async-start | bytes 1114112 | tf_op jit(solution)/shard_map/all_gather | solution.py:69
  230.6 119.7 %all-gather.13.cloned.1.call-start = ((), (), s32[]{:S(2)}) async-start(), calls=%async_computation.3 | async-start | bytes 1114112 | tf_op jit(solution)/shard_map/all_gather | solution.py:70
  365.5 14.4 %copy-start.2 = (bf16[2048,256]{1,0:T(8,128)(2,1)S(1)}, bf16[2048,256]{1,0:T(8,128)(2,1)}, u32[]{:S(2)}) copy-start(bf16[2048,256]{1,0:T(8,128)(2,1)} %get-tuple-element.17) | copy-start | bytes 3145732 | tf_op jit(solution)/shard_map/cond
Sparse Core Ops, SparseCore 0:
  11.1 67.3 all-gather.14
  81.5 62.2 all-gather.18
  146.9 62.2 all-gather.16
  233.6 56.2 all-gather.10
  292.8 57.4 all-gather.12
where the time goes:
time: 415 us; the launch traced here: 414 us
  waiting for transfers between devices  292 us (70%)
  matrix products  42.2 us (10%)
  starting transfers between devices  28.5 us (7%)
  other arithmetic  20 us (5%)
  local copies, waits for them, and re-layouts  16.9 us (4%)
  between operations  14.6 us (4%)
    all_to_all x1, waiting for transfers between devices, experts(): lax.all_to_all(outgoing, 'ep', split_axis=0, concat_axis=0, tiled=True)  99.4 us
    all_gather x1, waiting for transfers between devices, experts(): up_rows = lax.all_gather(w_up[0], 'ctx', axis=0, tiled=True)  65.4 us
    all_gather x1, waiting for transfers between devices, attend(): lax.all_gather(values[0], 'ctx', axis=0, tiled=True)  60.4 us
    all_gather x1, waiting for transfers between devices, attend(): lax.all_gather(keys[0], 'ctx', axis=0, tiled=True)  57.1 us
    dot_general x1, matrix products, compute(): jnp.einsum('gjrn,ngd->gjrd', exponent.astype(jnp.bfloat16), value_heads,...  15.9 us
    all_to_all x1, starting transfers between devices, experts(): lax.all_to_all(outgoing, 'ep', split_axis=0, concat_axis=0, tiled=True)  15.3 us
    reduce_sum x1, other arithmetic, compute(): new_totals = jnp.sum(exponent, axis=-1)  14.4 us
    dot_general x1, matrix products, compute(): jnp.einsum('rgjd,ngd->gjrn', group_rows, key_heads, preferred_element_typ...  13.2 us
  transfers between devices with their start and end apart: 7, of which 5 were waited for; matrix products, arithmetic and copies ran while one was open for 15% of the time, Pallas kernels for 0%

commit v1 on v0

--- a/solution.py
+++ b/solution.py
@@ -7,6 +7,24 @@
 HQ = 32
 KVH = 2
 DH = 128
+
+
+def ring_gather(value, axis, dim):
+    ways, here, step = (lax.axis_size(axis), lax.axis_index(axis), value.shape[dim])
+    shape = [n * ways if d == dim else n for d, n in enumerate(value.shape)]
+    full = lax.dynamic_update_slice_in_dim(
+        jnp.zeros(shape, value.dtype), value, here * step, axis=dim
+    )
+    going_up = going_down = value
+    for far in range(1, ways // 2 + 1):
+        going_up = lax.ppermute(going_up, axis, [(d, (d + 1) % ways) for d in range(ways)])
+        full = lax.dynamic_update_slice_in_dim(full, going_up, (here - far) % ways * step, axis=dim)
+        if 2 * far < ways:
+            going_down = lax.ppermute(going_down, axis, [(d, (d - 1) % ways) for d in range(ways)])
+            full = lax.dynamic_update_slice_in_dim(
+                full, going_down, (here + far) % ways * step, axis=dim
+            )
+    return full
 
 
 def attend(queries, keys, values):
@@ -65,10 +83,7 @@
 
     finals = update(
         initial,
-        (
-            lax.all_gather(keys[0], "ctx", axis=0, tiled=True),
-            lax.all_gather(values[0], "ctx", axis=0, tiled=True),
-        ),
+        (lax.all_gather(keys[0], "ctx", axis=0, tiled=True), ring_gather(values[0], "ctx", 0)),
         jnp.int32(0),
     )
     outputs = []

time: 415 us -> 383 us (0.923)
  waiting for transfers between devices: 292 us -> 182 us
  starting transfers between devices: 28.5 us -> 95.1 us
  local copies, waits for them, and re-layouts: 16.9 us -> 25.3 us
    ppermute x0 -> x15, starting transfers between devices: none -> 66.6 us  [the longest x7 50.6 us: ring_gather(): lax.ppermute(going_down, axis, [(d, (d - 1) % ways) for d in range(ways)])]
    all_gather x1 -> x0, waiting for transfers between devices: 60.4 us -> none  [attend(): lax.all_gather(values[0], 'ctx', axis=0, tiled=True)]
    all_gather x1, waiting for transfers between devices: 6.51 us -> 65.4 us  [experts(): down_rows = lax.all_gather(w_down[0], 'ctx', axis=0, tiled=True)]
    all_gather x1, waiting for transfers between devices: 65.4 us -> 6.54 us  [experts(): up_rows = lax.all_gather(w_up[0], 'ctx', axis=0, tiled=True)]
    all_gather x1, waiting for transfers between devices: 57.1 us -> 0.01 us  [attend(): lax.all_gather(keys[0], 'ctx', axis=0, tiled=True)]
    dynamic_update_slice x0 -> x16, local copies, waits for them, and re-layouts: none -> 9.04 us  [the longest x8 4.38 us: ring_gather(): lax.dynamic_update_slice_in_dim(full, going_up, (here - far) % ways * ste...]
    ppermute x0 -> x15, waiting for transfers between devices: none -> 8.07 us  [the longest x8 8.05 us: ring_gather(): lax.ppermute(going_up, axis, [(d, (d + 1) % ways) for d in range(ways)])]
  transfers between devices with their start and end apart: 7 -> 21, of which waited for: 5 -> 9; matrix products, arithmetic and copies ran while one was open for 15% -> 19% of each run, Pallas kernels for 0% -> 0%
where the time goes in v1:
time: 383 us; the launch traced here: 382 us
  waiting for transfers between devices  182 us (48%)
  starting transfers between devices  95.1 us (25%)
  matrix products  42.2 us (11%)
  local copies, waits for them, and re-layouts  25.3 us (7%)
  other arithmetic  21.2 us (6%)
  between operations  14.8 us (4%)
    all_to_all x1, waiting for transfers between devices, experts(): lax.all_to_all(outgoing, 'ep', split_axis=0, concat_axis=0, tiled=True)  99.4 us
    all_gather x1, waiting for transfers between devices, experts(): down_rows = lax.all_gather(w_down[0], 'ctx', axis=0, tiled=True)  65.4 us
    ppermute x7, starting transfers between devices, ring_gather(): lax.ppermute(going_down, axis, [(d, (d - 1) % ways) for d in range(ways)])  50.6 us
    ppermute x8, starting transfers between devices, ring_gather(): lax.ppermute(going_up, axis, [(d, (d + 1) % ways) for d in range(ways)])  16 us
    dot_general x1, matrix products, compute(): jnp.einsum('gjrn,ngd->gjrd', exponent.astype(jnp.bfloat16), value_heads,...  15.9 us
    all_to_all x1, starting transfers between devices, experts(): lax.all_to_all(outgoing, 'ep', split_axis=0, concat_axis=0, tiled=True)  15.3 us
    reduce_sum x1, other arithmetic, compute(): new_totals = jnp.sum(exponent, axis=-1)  14.3 us
    dot_general x1, matrix products, compute(): jnp.einsum('rgjd,ngd->gjrn', group_rows, key_heads, preferred_element_typ...  13.3 us
  transfers between devices with their start and end apart: 21, of which 9 were waited for; matrix products, arithmetic and copies ran while one was open for 19% of the time, Pallas kernels for 0%

profile of v1, /device:TPU:32, one launch (start us, length us, event | category | flops | bytes accessed | tf_op | source)
XLA Modules:
  0.0 381.5 jit_solution(2238488187018659361)
XLA Ops:
  15.4 15.3 %all-to-all-start = ((bf16[32,12,2048]{2,1,0:T(8,128)(2,1)}), bf16[32,12,2048]{2,1,0:T(8,128)(2,1)S(1)}, u32[]{:S(2)}, u32[]{:S(2)}) async-start(bf16[32,12,2048]{2,1,0:T(8,128)(2,1)} %reshape.205), calls=%async_computation | async-start | bytes 4194304 | tf_op jit(solution)/shard_map/all_to_all | solution.py:120
  31.5 99.4 %all-to-all-done = bf16[32,12,2048]{2,1,0:T(8,128)(2,1)S(1)} async-done(((bf16[32,12,2048]{2,1,0:T(8,128)(2,1)}), bf16[32,12,2048]{2,1,0:T(8,128)(2,1)S(1)}, u32[]{:S(2)}, u32[]{:S(2)}) %all-to-all-start) | async-done | bytes 1572896 | tf_op jit(solution)/shard_map/all_to_all | solution.py:120
  132.2 5.1 %fusion.15 = f32[384,768]{1,0:T(8,128)} fusion(bf16[384,2048]{1,0:T(8,128)(2,1)} %reshape.206, bf16[1,768,2048]{2,1,0:T(8,128)(2,1)} %all-gather.11.cloned.1.call-done), kind=kOutput, calls=%fused_computation.34 | convolution fusion | flops 1207959552 | bytes 5898240 | tf_op jit(solution)/shard_map/dot_general | solution.py:126
  137.3 6.5 %all-gather.13.cloned.1.call-done = bf16[1,768,2048]{2,1,0:T(8,128)(2,1)} async-done(((bf16[1,48,2048]{2,1,0:T(8,128)(2,1)}), bf16[1,768,2048]{2,1,0:T(8,128)(2,1)}) %all-gather.13.cloned.1.call-update) | async-done | bytes 3145744 | tf_op jit(solution)/shard_map/all_gather | solution.py:123
  143.8 65.4 %all-gather.15.cloned.1.call-done = bf16[1,768,2048]{2,1,0:T(8,128)(2,1)} async-done(((bf16[1,48,2048]{2,1,0:T(8,128)(2,1)}), bf16[1,768,2048]{2,1,0:T(8,128)(2,1)}) %all-gather.15.cloned.1.call-update) | async-done | bytes 3145744 | tf_op jit(solution)/shard_map/all_gather | solution.py:124
  209.2 6.3 %fusion.17 = bf16[384,2048]{1,0:T(8,128)(2,1)S(1)} fusion(bf16[1,768,2048]{2,1,0:T(8,128)(2,1)} %all-gather.15.cloned.1.call-done, bf16[384,2048]{1,0:T(8,128)(2,1)S(1)} %copy-done, bf16[1,768,2048]{2,1,0:T(8,128)(2,1)} %all-gather.13.cloned.1.call-done, f32[384,768]{1,0:T(8,128)} %fusion.15), kind=kOutput, calls=%fused_computation.36 | convolution fusion | flops 2418475008 | bytes 10616832 | tf_op jit(solution)/shard_map/dot_general | solution.py:129
  217.1 13.0 %all-to-all-start.1 = ((bf16[32,12,2048]{2,1,0:T(8,128)(2,1)}), bf16[32,12,2048]{2,1,0:T(8,128)(2,1)}, u32[]{:S(2)}, u32[]{:S(2)}) async-start(bf16[32,12,2048]{2,1,0:T(8,128)(2,1)} %reshape.207), calls=%async_computation.1 | async-start | bytes 4194304 | tf_op jit(solution)/shard_map/all_to_all | solution.py:131
  230.8 2.6 collective-permute-start
  233.4 6.5 %collective-permute-start.1 = (bf16[128,256]{0,1:T(8,128)(2,1)S(1)}, bf16[128,256]{0,1:T(8,128)(2,1)S(1)}, u32[]{:S(2)}, u32[]{:S(2)}) collective-permute-start(bf16[128,256]{0,1:T(8,128)(2,1)S(1)} %bitcast.104), channel_id=1, source_target_pairs={{0,480},{32,0},{64,32},{96,64},{128,96},{160,128},{192,160},{224,1... | collective-permute-start | bytes 196616 | tf_op jit(solution)/shard_map/ppermute | solution.py:23
  240.3 1.9 collective-permute-start.2
  242.2 7.2 %collective-permute-start.3 = (bf16[128,256]{0,1:T(8,128)(2,1)S(1)}, bf16[128,256]{0,1:T(8,128)(2,1)S(1)}, u32[]{:S(2)}, u32[]{:S(2)}) collective-permute-start(bf16[128,256]{0,1:T(8,128)(2,1)S(1)} %collective-permute-done.1), channel_id=1, source_target_pairs={{0,480},{32,0},{64,32},{96,64},{128,96},{160,128},{192,160},{224,1... | collective-permute-start | bytes 196616 | tf_op jit(solution)/shard_map/ppermute | solution.py:23
  251.7 7.5 %collective-permute-start.5 = (bf16[128,256]{0,1:T(8,128)(2,1)S(1)}, bf16[128,256]{0,1:T(8,128)(2,1)S(1)}, u32[]{:S(2)}, u32[]{:S(2)}) collective-permute-start(bf16[128,256]{0,1:T(8,128)(2,1)S(1)} %collective-permute-done.3), channel_id=1, source_target_pairs={{0,480},{32,0},{64,32},{96,64},{128,96},{160,128},{192,160},{224,1... | collective-permute-start | bytes 196616 | tf_op jit(solution)/shard_map/ppermute | solution.py:23
  261.4 7.2 %collective-permute-start.7 = (bf16[128,256]{0,1:T(8,128)(2,1)S(1)}, bf16[128,256]{0,1:T(8,128)(2,1)S(1)}, u32[]{:S(2)}, u32[]{:S(2)}) collective-permute-start(bf16[128,256]{0,1:T(8,128)(2,1)S(1)} %collective-permute-done.5), channel_id=1, source_target_pairs={{0,480},{32,0},{64,32},{96,64},{128,96},{160,128},{192,160},{224,1... | collective-permute-start | bytes 196616 | tf_op jit(solution)/shard_map/ppermute | solution.py:23
  268.8 1.9 collective-permute-start.8
  270.8 7.4 %collective-permute-start.9 = (bf16[128,256]{0,1:T(8,128)(2,1)S(1)}, bf16[128,256]{0,1:T(8,128)(2,1)S(1)}, u32[]{:S(2)}, u32[]{:S(2)}) collective-permute-start(bf16[128,256]{0,1:T(8,128)(2,1)S(1)} %collective-permute-done.7), channel_id=1, source_target_pairs={{0,480},{32,0},{64,32},{96,64},{128,96},{160,128},{192,160},{224,1... | collective-permute-start | bytes 196616 | tf_op jit(solution)/shard_map/ppermute | solution.py:23
  282.3 7.2 %collective-permute-start.11 = (bf16[128,256]{0,1:T(8,128)(2,1)S(1)}, bf16[128,256]{0,1:T(8,128)(2,1)S(1)}, u32[]{:S(2)}, u32[]{:S(2)}) collective-permute-start(bf16[128,256]{0,1:T(8,128)(2,1)S(1)} %collective-permute-done.9), channel_id=1, source_target_pairs={{0,480},{32,0},{64,32},{96,64},{128,96},{160,128},{192,160},{224,1... | collective-permute-start | bytes 196616 | tf_op jit(solution)/shard_map/ppermute | solution.py:23
  289.5 1.9 collective-permute-start.12
  291.5 7.5 %collective-permute-start.13 = (bf16[128,256]{0,1:T(8,128)(2,1)S(1)}, bf16[128,256]{0,1:T(8,128)(2,1)S(1)}, u32[]{:S(2)}, u32[]{:S(2)}) collective-permute-start(bf16[128,256]{0,1:T(8,128)(2,1)S(1)} %collective-permute-done.11), channel_id=1, source_target_pairs={{0,480},{32,0},{64,32},{96,64},{128,96},{160,128},{192,160},{224,1... | collective-permute-start | bytes 196616 | tf_op jit(solution)/shard_map/ppermute | solution.py:23
  301.5 7.0 %collective-permute-done.14 = bf16[128,256]{0,1:T(8,128)(2,1)S(1)} collective-permute-done((bf16[128,256]{0,1:T(8,128)(2,1)S(1)}, bf16[128,256]{0,1:T(8,128)(2,1)S(1)}, u32[]{:S(2)}, u32[]{:S(2)}) %collective-permute-start.14) | collective-permute-done | bytes 65568 | tf_op jit(solution)/shard_map/ppermute | solution.py:20
  308.5 55.9 %conditional.1 = (f32[2,16,128]{2,1,0:T(8,128)S(1)}, f32[2,16,128,128]{3,2,1,0:T(8,128)S(1)}) conditional(s32[]{:T(128)} %convert_element_type.87, () %tuple.159, (s32[2048]{0:T(1024)S(1)}, s32[128]{0:T(128)}, bf16[2048,256]{1,0:T(8,128)(2,1)}, bf16[1,128,4096]{2,1,0:T(8,128)(2,1)S(1)}, s32[]{:T(128)}, ...), branch_computations={%region_1.2_spmd, %region_2.5_spmd.clone.clone} | conditional | flops 4387500032 | bytes 129871256 | solution.py:81
  320.6 13.3 %fusion.2 = (f32[2,16,128]{2,1,0:T(8,128)S(1)}, f32[2,2048,128,16]{2,1,3,0:T(8,128)}) fusion(pred[128,2048]{0,1:T(8,128)(4,1)S(1)} %broadcast_compare_fusion, bf16[128,2,16,128]{3,2,1,0:T(8,128)(2,1)S(1)} %bitcast.99, bf16[2048,2,128,1]{2,1,0,3:T(2,128)(2,1)S(1)} %bitcast.98), kind=kOutput, calls=%fused_computation.5 | convolution fusion | flops 2172645376 | bytes 35930112 | tf_op jit(solution)/shard_map/cond/branch_1_fun/rgjd,ngd->gjrn/dot_general | solution.py:60
  333.9 15.9 %fusion.3 = f32[2,16,128,128]{3,2,1,0:T(8,128)S(1)} fusion(bf16[2048,2,128,1]{0,2,3,1:T(8,128)(2,1)S(1)} %bitcast.102, f32[2,2048,128,16]{2,1,3,0:T(8,128)} %get-tuple-element.1491, f32[2,16,128]{2,1,0:T(8,128)S(1)} %broadcast_maximum_fusion, pred[128,2048]{0,1:T(8,128)(4,1)S(1)} %broadcast_compare_fusion), kind=kOutput, calls=%fused_computation.6 | convolution fusion | flops 2181038080 | bytes 36978688 | tf_op jit(solution)/shard_map/cond/branch_1_fun/gjrn,ngd->gjrd/dot_general | solution.py:70
  349.8 14.3 %fusion.1 = f32[2,16,128]{2,1,0:T(8,128)S(1)} fusion(f32[2,2048,128,16]{2,1,3,0:T(8,128)} %get-tuple-element.1491, f32[2,16,128]{2,1,0:T(8,128)S(1)} %broadcast_maximum_fusion, pred[128,2048]{0,1:T(8,128)(4,1)S(1)} %broadcast_compare_fusion), kind=kLoop, calls=%fused_computation.4 | loop fusion | flops 33550336 | bytes 33849344 | tf_op jit(solution)/shard_map/cond/branch_1_fun/reduce_sum | solution.py:69
  367.1 2.5 reshape.208
  (125 shorter events, 42.8 us)
Async XLA Ops:
  7.2 125.1 %all-gather.11.cloned.1.call-start = ((), (), s32[]{:S(2)}) async-start(), calls=%async_computation.3 | async-start | bytes 3342336 | tf_op jit(solution)/shard_map/all_gather | solution.py:122
  7.9 135.9 %all-gather.13.cloned.1.call-start = ((), (), s32[]{:S(2)}) async-start(), calls=%async_computation.4 | async-start | bytes 3342336 | tf_op jit(solution)/shard_map/all_gather | solution.py:123
  15.4 115.5 %all-to-all-start = ((bf16[32,12,2048]{2,1,0:T(8,128)(2,1)}), bf16[32,12,2048]{2,1,0:T(8,128)(2,1)S(1)}, u32[]{:S(2)}, u32[]{:S(2)}) async-start(bf16[32,12,2048]{2,1,0:T(8,128)(2,1)} %reshape.205), calls=%async_computation | async-start | bytes 4194304 | tf_op jit(solution)/shard_map/all_to_all | solution.py:120
  30.7 178.5 %all-gather.15.cloned.1.call-start = ((), (), s32[]{:S(2)}) async-start(), calls=%async_computation.5 | async-start | bytes 3342336 | tf_op jit(solution)/shard_map/all_gather | solution.py:124
  132.2 77.0 %copy-start = (bf16[384,2048]{1,0:T(8,128)(2,1)S(1)}, bf16[384,2048]{1,0:T(8,128)(2,1)}, u32[]{:S(2)}) copy-start(bf16[384,2048]{1,0:T(8,128)(2,1)} %reshape.206) | copy-start | bytes 4718596
  217.1 63.2 %copy-start.19 = (f32[1,128,2]{1,2,0:T(2,128)S(1)}, f32[1,128,2]{1,2,0:T(2,128)}, u32[]{:S(2)}) copy-start(f32[1,128,2]{1,2,0:T(2,128)} %param.17) | copy-start | bytes 3076
  217.1 91.4 %copy-start.1 = (bf16[1,128,4096]{2,1,0:T(8,128)(2,1)S(1)}, bf16[1,128,4096]{2,1,0:T(8,128)(2,1)}, u32[]{:S(2)}) copy-start(bf16[1,128,4096]{2,1,0:T(8,128)(2,1)} %param.12) | copy-start | bytes 3145732
  217.1 150.0 %all-to-all-start.1 = ((bf16[32,12,2048]{2,1,0:T(8,128)(2,1)}), bf16[32,12,2048]{2,1,0:T(8,128)(2,1)}, u32[]{:S(2)}, u32[]{:S(2)}) async-start(bf16[32,12,2048]{2,1,0:T(8,128)(2,1)} %reshape.207), calls=%async_computation.1 | async-start | bytes 4194304 | tf_op jit(solution)/shard_map/all_to_all | solution.py:131
  230.1 78.4 %all-gather.9.cloned.1.call-start = ((), (), s32[]{:S(2)}) async-start(), calls=%async_computation.2 | async-start | bytes 1114112 | tf_op jit(solution)/shard_map/all_gather | solution.py:86
  230.8 9.5 %collective-permute-start = (bf16[128,256]{0,1:T(8,128)(2,1)S(1)}, bf16[128,256]{0,1:T(8,128)(2,1)S(1)}, u32[]{:S(2)}, u32[]{:S(2)}) collective-permute-start(bf16[128,256]{0,1:T(8,128)(2,1)S(1)} %bitcast.103), channel_id=1, source_target_pairs={{0,32},{32,64},{64,96},{96,128},{128,160},{160,192},{192,224},{224... | collective-permute-start | bytes 196616 | tf_op jit(solution)/shard_map/ppermute | solution.py:20
  233.4 8.8 %collective-permute-start.1 = (bf16[128,256]{0,1:T(8,128)(2,1)S(1)}, bf16[128,256]{0,1:T(8,128)(2,1)S(1)}, u32[]{:S(2)}, u32[]{:S(2)}) collective-permute-start(bf16[128,256]{0,1:T(8,128)(2,1)S(1)} %bitcast.104), channel_id=1, source_target_pairs={{0,480},{32,0},{64,32},{96,64},{128,96},{160,128},{192,160},{224,1... | collective-permute-start | bytes 196616 | tf_op jit(solution)/shard_map/ppermute | solution.py:23
  240.3 9.5 %collective-permute-start.2 = (bf16[128,256]{0,1:T(8,128)(2,1)S(1)}, bf16[128,256]{0,1:T(8,128)(2,1)S(1)}, u32[]{:S(2)}, u32[]{:S(2)}) collective-permute-start(bf16[128,256]{0,1:T(8,128)(2,1)S(1)} %collective-permute-done), channel_id=1, source_target_pairs={{0,32},{32,64},{64,96},{96,128},{128,160},{160,192},{192,224},{224... | collective-permute-start | bytes 196616 | tf_op jit(solution)/shard_map/ppermute | solution.py:20
  242.2 9.5 %collective-permute-start.3 = (bf16[128,256]{0,1:T(8,128)(2,1)S(1)}, bf16[128,256]{0,1:T(8,128)(2,1)S(1)}, u32[]{:S(2)}, u32[]{:S(2)}) collective-permute-start(bf16[128,256]{0,1:T(8,128)(2,1)S(1)} %collective-permute-done.1), channel_id=1, source_target_pairs={{0,480},{32,0},{64,32},{96,64},{128,96},{160,128},{192,160},{224,1... | collective-permute-start | bytes 196616 | tf_op jit(solution)/shard_map/ppermute | solution.py:23
  249.7 9.6 %collective-permute-start.4 = (bf16[128,256]{0,1:T(8,128)(2,1)S(1)}, bf16[128,256]{0,1:T(8,128)(2,1)S(1)}, u32[]{:S(2)}, u32[]{:S(2)}) collective-permute-start(bf16[128,256]{0,1:T(8,128)(2,1)S(1)} %collective-permute-done.2), channel_id=1, source_target_pairs={{0,32},{32,64},{64,96},{96,128},{128,160},{160,192},{192,224},{224... | collective-permute-start | bytes 196616 | tf_op jit(solution)/shard_map/ppermute | solution.py:20
  251.7 9.8 %collective-permute-start.5 = (bf16[128,256]{0,1:T(8,128)(2,1)S(1)}, bf16[128,256]{0,1:T(8,128)(2,1)S(1)}, u32[]{:S(2)}, u32[]{:S(2)}) collective-permute-start(bf16[128,256]{0,1:T(8,128)(2,1)S(1)} %collective-permute-done.3), channel_id=1, source_target_pairs={{0,480},{32,0},{64,32},{96,64},{128,96},{160,128},{192,160},{224,1... | collective-permute-start | bytes 196616 | tf_op jit(solution)/shard_map/ppermute | solution.py:23
  259.4 9.5 %collective-permute-start.6 = (bf16[128,256]{0,1:T(8,128)(2,1)S(1)}, bf16[128,256]{0,1:T(8,128)(2,1)S(1)}, u32[]{:S(2)}, u32[]{:S(2)}) collective-permute-start(bf16[128,256]{0,1:T(8,128)(2,1)S(1)} %collective-permute-done.4), channel_id=1, source_target_pairs={{0,32},{32,64},{64,96},{96,128},{128,160},{160,192},{192,224},{224... | collective-permute-start | bytes 196616 | tf_op jit(solution)/shard_map/ppermute | solution.py:20
  261.4 9.3 %collective-permute-start.7 = (bf16[128,256]{0,1:T(8,128)(2,1)S(1)}, bf16[128,256]{0,1:T(8,128)(2,1)S(1)}, u32[]{:S(2)}, u32[]{:S(2)}) collective-permute-start(bf16[128,256]{0,1:T(8,128)(2,1)S(1)} %collective-permute-done.5), channel_id=1, source_target_pairs={{0,480},{32,0},{64,32},{96,64},{128,96},{160,128},{192,160},{224,1... | collective-permute-start | bytes 196616 | tf_op jit(solution)/shard_map/ppermute | solution.py:23
  268.8 9.5 %collective-permute-start.8 = (bf16[128,256]{0,1:T(8,128)(2,1)S(1)}, bf16[128,256]{0,1:T(8,128)(2,1)S(1)}, u32[]{:S(2)}, u32[]{:S(2)}) collective-permute-start(bf16[128,256]{0,1:T(8,128)(2,1)S(1)} %collective-permute-done.6), channel_id=1, source_target_pairs={{0,32},{32,64},{64,96},{96,128},{128,160},{160,192},{192,224},{224... | collective-permute-start | bytes 196616 | tf_op jit(solution)/shard_map/ppermute | solution.py:20
  270.8 11.5 %collective-permute-start.9 = (bf16[128,256]{0,1:T(8,128)(2,1)S(1)}, bf16[128,256]{0,1:T(8,128)(2,1)S(1)}, u32[]{:S(2)}, u32[]{:S(2)}) collective-permute-start(bf16[128,256]{0,1:T(8,128)(2,1)S(1)} %collective-permute-done.7), channel_id=1, source_target_pairs={{0,480},{32,0},{64,32},{96,64},{128,96},{160,128},{192,160},{224,1... | collective-permute-start | bytes 196616 | tf_op jit(solution)/shard_map/ppermute | solution.py:23
  278.3 11.2 %collective-permute-start.10 = (bf16[128,256]{0,1:T(8,128)(2,1)S(1)}, bf16[128,256]{0,1:T(8,128)(2,1)S(1)}, u32[]{:S(2)}, u32[]{:S(2)}) collective-permute-start(bf16[128,256]{0,1:T(8,128)(2,1)S(1)} %collective-permute-done.8), channel_id=1, source_target_pairs={{0,32},{32,64},{64,96},{96,128},{128,160},{160,192},{192,224},{224... | collective-permute-start | bytes 196616 | tf_op jit(solution)/shard_map/ppermute | solution.py:20
  282.3 9.2 %collective-permute-start.11 = (bf16[128,256]{0,1:T(8,128)(2,1)S(1)}, bf16[128,256]{0,1:T(8,128)(2,1)S(1)}, u32[]{:S(2)}, u32[]{:S(2)}) collective-permute-start(bf16[128,256]{0,1:T(8,128)(2,1)S(1)} %collective-permute-done.9), channel_id=1, source_target_pairs={{0,480},{32,0},{64,32},{96,64},{128,96},{160,128},{192,160},{224,1... | collective-permute-start | bytes 196616 | tf_op jit(solution)/shard_map/ppermute | solution.py:23
  289.5 9.5 %collective-permute-start.12 = (bf16[128,256]{0,1:T(8,128)(2,1)S(1)}, bf16[128,256]{0,1:T(8,128)(2,1)S(1)}, u32[]{:S(2)}, u32[]{:S(2)}) collective-permute-start(bf16[128,256]{0,1:T(8,128)(2,1)S(1)} %collective-permute-done.10), channel_id=1, source_target_pairs={{0,32},{32,64},{64,96},{96,128},{128,160},{160,192},{192,224},{224... | collective-permute-start | bytes 196616 | tf_op jit(solution)/shard_map/ppermute | solution.py:20
  291.5 10.0 %collective-permute-start.13 = (bf16[128,256]{0,1:T(8,128)(2,1)S(1)}, bf16[128,256]{0,1:T(8,128)(2,1)S(1)}, u32[]{:S(2)}, u32[]{:S(2)}) collective-permute-start(bf16[128,256]{0,1:T(8,128)(2,1)S(1)} %collective-permute-done.11), channel_id=1, source_target_pairs={{0,480},{32,0},{64,32},{96,64},{128,96},{160,128},{192,160},{224,1... | collective-permute-start | bytes 196616 | tf_op jit(solution)/shard_map/ppermute | solution.py:23
  299.0 9.5 %collective-permute-start.14 = (bf16[128,256]{0,1:T(8,128)(2,1)S(1)}, bf16[128,256]{0,1:T(8,128)(2,1)S(1)}, u32[]{:S(2)}, u32[]{:S(2)}) collective-permute-start(bf16[128,256]{0,1:T(8,128)(2,1)S(1)} %collective-permute-done.12), channel_id=1, source_target_pairs={{0,32},{32,64},{64,96},{96,128},{128,160},{160,192},{192,224},{224... | collective-permute-start | bytes 196616 | tf_op jit(solution)/shard_map/ppermute | solution.py:20
  (17 other events, 66.9 us)
Sparse Core Ops, SparseCore 0:
  11.1 67.3 all-gather.10
  81.5 62.2 all-gather.12
  146.9 62.2 all-gather.14
  233.6 57.4 all-gather.8
